TPU v7x, 32 devices: a whole 2x2x4 slice. The times are simulated.
32 devices in a mesh: groups: 2 (over y), ctx: 16 (over z, x, core).
Axes of the slice: x: 2, y: 2, z: 4, core: 2. Of those that a mesh axis runs over, the one named last changes fastest.
Arguments:
- queries: bfloat16 [12288, 1024], P(('groups', 'ctx')), parts along dimension 0, may hold values from -14 to 14
- inputs: bfloat16 [12288, 1024], P(('groups', 'ctx')), parts along dimension 0, may hold values from -6 to 6
- w_kv: bfloat16 [1024, 2048], replicated, may hold values from -1 to 1
- rand_blocks: int32 [192, 3], P('groups'), parts along dimension 0, may hold values from 1 to 94, as said below
- w_cross: bfloat16 [1024, 2048], replicated, may hold values from -1 to 1
- vocab_table: bfloat16 [6144, 1024], P('ctx'), may hold values from -14 to 14
- summary_ids: int32 [512], P('groups'), parts along dimension 0, may hold values from 0 to 6143
Outputs:
- attended: bfloat16 [12288, 1024], P(('groups', 'ctx')), parts along dimension 0
- summary: bfloat16 [512, 1024], P(('groups', 'ctx')), parts along dimension 0
There are 2 independent parts, one for each index of `groups`. A program takes and returns all parts, laid end to end along the dimension named above; an argument that names none is the same for every part. Nothing has to cross between parts.
Inputs may be any that keep to these rules, and one draw needn't show every extreme that they name: `rand_blocks`: take each run of 6 query blocks that starts at a multiple of 6: its 18 random blocks never lie in its own run (they may lie in any other run, and may repeat a block of the window), the 3 blocks of one query block lie in different runs, at most 2 of them lie in any one other run and some run holds exactly 2 of them. No random block is block 0 or block 95.
All inputs are finite; a program needn't handle non-finite values.
Results may differ from a plain program's by a relative error of at most 0.0075.
Values may be sent and summed in bfloat16 or wider, within the bound.
A program may use at most 192 MiB of HBM per device.

v0:
```python
import jax
import jax.numpy as jnp
from jax import lax
from jax.sharding import PartitionSpec as P

HEADS = 16
HEAD = 64
BLOCK = 64
MASKED_SCORE = -1e30


def from_root(block, axis, holder):
    block = jnp.where(lax.axis_index(axis) == holder, block, jnp.zeros_like(block))
    return lax.psum(block, axis)


def padded_2(x, sides, width):
    for axis, dim in sides:
        size, length = (lax.axis_size(axis), x.shape[dim])
        up = [(i, (i + 1) % size) for i in range(size - 1)]
        down = [(j, i) for i, j in up]
        last = lax.slice_in_dim(x, length - width, length, axis=dim)
        initial = lax.slice_in_dim(x, 0, width, axis=dim)
        before = lax.ppermute(last, axis, up)
        after = lax.ppermute(initial, axis, down)
        x = jnp.concatenate([before, x, after], axis=dim)
    return x


def partial_rows(query_rows, key_rows, value_rows):
    row_count = query_rows.shape[0]
    key_count = key_rows.shape[0]
    scores = jnp.einsum(
        "qhe,khe->qhk",
        query_rows.reshape(row_count, HEADS, HEAD),
        key_rows.reshape(key_count, HEADS, HEAD),
        preferred_element_type=jnp.float32,
    ) * HEAD ** (-0.5)
    peak = jnp.max(scores, axis=2)
    weights = jnp.exp(scores - peak[:, :, None])
    totals = jnp.sum(weights, axis=2)
    sums = jnp.einsum(
        "qhk,khe->qhe",
        weights,
        value_rows.reshape(key_count, HEADS, HEAD).astype(jnp.float32),
        precision=lax.Precision.HIGHEST,
    )
    return (peak, totals, sums.reshape(row_count, HEADS * HEAD))


def rescale(sums, scaling):
    row_count = sums.shape[0]
    return (sums.reshape(row_count, HEADS, HEAD) * scaling[:, :, None]).reshape(
        row_count, HEADS * HEAD
    )


def normalize(totals, sums):
    row_count = sums.shape[0]
    return (sums.reshape(row_count, HEADS, HEAD) / totals[:, :, None]).reshape(
        row_count, HEADS * HEAD
    )


def global_block(queries, key_value, root, start):
    query_piece = lax.slice_in_dim(queries, start, start + BLOCK, axis=0)
    pair_piece = lax.slice_in_dim(key_value, start, start + BLOCK, axis=0)
    return (from_root(query_piece, "ctx", root), from_root(pair_piece, "ctx", root))


def local(queries, inputs, w_kv, rand_blocks, w_cross, vocab_table, summary_ids):
    devices = lax.axis_size("ctx")
    position = lax.axis_index("ctx")
    row_count, feature_count = inputs.shape
    block_count = row_count // BLOCK
    pick_count = rand_blocks.shape[1]
    total_blocks = block_count * devices
    key_value = jnp.dot(inputs, w_kv, preferred_element_type=jnp.float32).astype(jnp.bfloat16)
    padded_inputs = padded_2(inputs, (("ctx", 0),), BLOCK)
    rim_rows = jnp.concatenate([padded_inputs[:BLOCK], padded_inputs[row_count + BLOCK :]], axis=0)
    rim_pairs = jnp.dot(rim_rows, w_kv, preferred_element_type=jnp.float32).astype(jnp.bfloat16)
    padded = jnp.concatenate([rim_pairs[:BLOCK], key_value, rim_pairs[BLOCK:]], axis=0)
    first_query, first_pair = global_block(queries, key_value, 0, 0)
    last_query, last_pair = global_block(queries, key_value, devices - 1, row_count - BLOCK)
    request_count = pick_count * block_count
    slot_count = (request_count + devices - 2) // (devices - 1)
    requests = rand_blocks.reshape(devices, request_count)
    owners = requests // block_count
    within = requests % block_count
    order = jnp.arange(request_count, dtype=jnp.int32)
    earlier = order[None, :] < order[:, None]
    matching = owners[:, :, None] == owners[:, None, :]
    ranks = jnp.sum(jnp.logical_and(matching, earlier[None, :, :]), axis=2)
    slot_ids = jnp.arange(slot_count, dtype=jnp.int32)
    served = jnp.logical_and(
        (owners == position)[:, None, :], ranks[:, None, :] == slot_ids[None, :, None]
    )
    sources = jnp.sum(jnp.where(served, within[:, None, :], 0), axis=2)
    filled = jnp.any(served, axis=2)
    outgoing = inputs.reshape(block_count, BLOCK, feature_count)[sources]
    outgoing = jnp.where(filled[:, :, None, None], outgoing, jnp.zeros((), jnp.bfloat16))
    arrived = lax.all_to_all(outgoing, "ctx", split_axis=0, concat_axis=0, tiled=True)
    my_owners = lax.dynamic_index_in_dim(owners, position, 0, keepdims=False)
    my_ranks = lax.dynamic_index_in_dim(ranks, position, 0, keepdims=False)
    fetched = arrived.reshape(devices * slot_count, BLOCK, feature_count)[
        my_owners * slot_count + my_ranks
    ]
    far_pairs = jnp.dot(
        fetched.reshape(request_count * BLOCK, feature_count),
        w_kv,
        preferred_element_type=jnp.float32,
    ).astype(jnp.bfloat16)
    far_pairs = far_pairs.reshape(block_count, pick_count * BLOCK, 2 * feature_count)
    framed = padded.reshape(block_count + 2, BLOCK, 2 * feature_count)
    window = jnp.concatenate(
        [framed[:block_count], framed[1 : block_count + 1], framed[2:]], axis=1
    )
    end_pairs = jnp.concatenate([first_pair, last_pair], axis=0)
    end_pairs = jnp.broadcast_to(end_pairs[None], (block_count, 2 * BLOCK, 2 * feature_count))
    key_sets = jnp.concatenate([window, end_pairs, far_pairs], axis=1)
    span = key_sets.shape[1]
    numbers = position * block_count + jnp.arange(block_count, dtype=jnp.int32)
    flags = jnp.stack(
        [numbers >= 2, jnp.ones((block_count,), dtype=bool), numbers <= total_blocks - 3], axis=1
    )
    valid = jnp.concatenate(
        [jnp.repeat(flags, BLOCK, axis=1), jnp.ones((block_count, span - 3 * BLOCK), dtype=bool)],
        axis=1,
    )
    query_blocks = queries.reshape(block_count, BLOCK, HEADS, HEAD)
    key_blocks = key_sets[:, :, :feature_count].reshape(block_count, span, HEADS, HEAD)
    value_blocks = key_sets[:, :, feature_count:].reshape(block_count, span, HEADS, HEAD)
    scores = jnp.einsum(
        "bqhe,bkhe->bhqk", query_blocks, key_blocks, preferred_element_type=jnp.float32
    ) * HEAD ** (-0.5)
    scores = jnp.where(valid[:, None, None, :], scores, MASKED_SCORE)
    weights = jnp.exp(scores - jnp.max(scores, axis=3, keepdims=True))
    probs = (weights / jnp.sum(weights, axis=3, keepdims=True)).astype(jnp.bfloat16)
    sparse_out = jnp.einsum(
        "bhqk,bkhe->bqhe", probs, value_blocks, preferred_element_type=jnp.float32
    )
    sparse_out = sparse_out.reshape(block_count, BLOCK, feature_count)
    end_queries = jnp.concatenate([first_query, last_query], axis=0)
    end_peak, end_totals, end_sums = partial_rows(
        end_queries, key_value[:, :feature_count], key_value[:, feature_count:]
    )
    shard_rows = vocab_table.shape[0]
    offsets = summary_ids - position * shard_rows
    inside = jnp.logical_and(offsets >= 0, offsets < shard_rows)
    looked = vocab_table[jnp.clip(offsets, 0, shard_rows - 1)].astype(jnp.float32)
    looked = jnp.where(inside[:, None], looked, 0.0)
    end_top = lax.pmax(end_peak, "ctx")
    end_scale = jnp.exp(end_peak - end_top)
    global_sums, global_totals, gathered_rows = lax.psum(
        (rescale(end_sums, end_scale), end_totals * end_scale, looked), "ctx"
    )
    global_out = normalize(global_totals, global_sums)
    sparse_out = sparse_out.at[0].set(jnp.where(position == 0, global_out[:BLOCK], sparse_out[0]))
    sparse_out = sparse_out.at[block_count - 1].set(
        jnp.where(position == devices - 1, global_out[BLOCK:], sparse_out[block_count - 1])
    )
    attended = sparse_out.reshape(row_count, feature_count).astype(jnp.bfloat16)
    encoded = (inputs.astype(jnp.float32) + attended.astype(jnp.float32)).astype(jnp.bfloat16)
    cross = jnp.dot(encoded, w_cross, preferred_element_type=jnp.float32).astype(jnp.bfloat16)
    summary_queries = gathered_rows.astype(jnp.bfloat16)
    cross_peak, cross_totals, cross_sums = partial_rows(
        summary_queries, cross[:, :feature_count], cross[:, feature_count:]
    )
    share = summary_queries.shape[0] // devices
    top_scores = lax.pmax(cross_peak, "ctx")
    scaling = jnp.exp(cross_peak - top_scores)
    scaled_sums = rescale(cross_sums, scaling)
    whole_sums, whole_totals = lax.psum((scaled_sums, cross_totals * scaling), "ctx")
    summary = lax.dynamic_slice_in_dim(
        normalize(whole_totals, whole_sums), position * share, share, 0
    )
    return (attended, summary.astype(jnp.bfloat16))


def solution(mesh):
    return jax.shard_map(
        local,
        mesh=mesh,
        in_specs=(
            P(("groups", "ctx"), None),
            P(("groups", "ctx"), None),
            P(),
            P("groups", None),
            P(),
            P("ctx", None),
            P("groups"),
        ),
        out_specs=(P(("groups", "ctx"), None), P(("groups", "ctx"), None)),
        check_vma=False,
    )
```

profile of v0, /device:TPU:0, one launch (start us, length us, event | category | flops | bytes accessed | tf_op | source)
XLA Modules:
  0.0 558.2 jit_solution(12927445662915458482)
XLA Ops:
  7.2 0.8 broadcast_divide_fusion.1
  7.9 0.7 sign_compare_fusion
  9.3 0.5 convert_reduce_fusion
  10.4 3.9 gather_fusion
  14.3 4.5 broadcast_select_fusion
  18.8 7.5 %all-to-all-start = ((bf16[16,2,64,1024]{3,2,1,0:T(8,128)(2,1)}), bf16[16,2,64,1024]{3,2,1,0:T(8,128)(2,1)}, u32[]{:S(2)}, u32[]{:S(2)}) async-start(bf16[16,2,64,1024]{3,2,1,0:T(8,128)(2,1)} %broadcast_select_fusion), calls=%async_computation | async-start | bytes 8388608 | tf_op jit(solution)/shard_map/all_to_all | solution.py:102
  26.4 0.7 fusion.64
  27.0 2.3 collective-permute-start
  29.3 1.3 collective-permute-start.1
  30.6 1.7 slice_select_fusion.4
  32.3 4.0 convolution_convert_fusion.2
  36.3 0.8 slice_select_fusion.2
  37.2 0.7 compare_select_fusion
  37.9 0.6 pad_clamp_fusion
  38.5 2.1 gather_fusion.2
  40.7 0.7 compare_and_fusion
  41.4 0.6 pad_add_fusion
  42.1 2.2 convert_select_fusion
  44.2 1.3 fusion.63
  45.5 0.5 fusion.53
  46.0 1.9 reshape.293
  47.9 1.5 copy.112
  49.4 2.3 copy.111
  51.7 0.8 broadcast_in_dim.59
  52.6 2.9 convolution_convert_fusion.3
  55.6 0.4 pad_maximum_fusion
  56.0 1.3 constant_dynamic-update-slice_fusion.3
  57.3 1.3 constant_dynamic-update-slice_fusion.2
  58.7 1.4 constant_dynamic-update-slice_fusion.1
  60.1 124.6 %all-reduce.12.cloned.1.call-done = (bf16[64,2048]{1,0:T(8,128)(2,1)}, bf16[64,2048]{1,0:T(8,128)(2,1)}, bf16[64,1024]{1,0:T(8,128)(2,1)}, bf16[64,1024]{1,0:T(8,128)(2,1)}) async-done(((bf16[64,2048]{1,0:T(8,128)(2,1)}, bf16[64,2048]{1,0:T(8,128)(2,1)}, bf16[64,1024]{1,0:T(8,128)(2,1)}, bf16[64,1024]{1,0:T(8,128)(2,1)}), (bf16[64,2048]{1,0:T(8,128)(2,1)}, bf16[64,2048]{1,0:T(8,128)(2,1)}, ...) | async-done | bytes 786448 | tf_op jit(solution)/shard_map/psum | solution.py:14
  184.7 1.1 pad_maximum_fusion.3
  185.9 2.3 bitcast_reduce_fusion.2
  188.2 30.9 %pmax.14 = f32[128,16]{0,1:T(8,128)S(1)} all-reduce(f32[128,16]{0,1:T(8,128)S(1)} %get-tuple-element.68), channel_id=1, replica_groups=mesh['groups'=2,'ctx'=16] {'ctx'}, use_global_device_ids=true, to_apply=%region_10.11 | all-reduce | flops 2048 | bytes 16384 | tf_op jit(solution)/shard_map/pmax | solution.py:152
  219.1 2.6 fusion.18
  222.0 2.5 fusion.39
  224.6 1.0 pad_maximum_fusion.2
  225.6 2.1 broadcast_dynamic-update-slice_fusion
  227.7 70.7 %all-reduce.13 = (f32[128,16]{0,1:T(8,128)S(1)}, bf16[256,1024]{1,0:T(8,128)(2,1)S(1)}) all-reduce(f32[128,16]{0,1:T(8,128)S(1)} %get-tuple-element.42, f32[256,1024]{1,0:T(8,128)S(1)} %copy-done.4), channel_id=1, replica_groups=mesh['groups'=2,'ctx'=16] {'ctx'}, use_global_device_ids=true, to_apply=%region_13.14 | all-reduce | flops 264192 | bytes 1589248 | tf_op jit(solution)/shard_map/psum | solution.py:154
  298.4 1.0 copy.120
  299.4 13.7 %all-reduce.8.cloned.1.call-done = f32[128,16,64]{0,2,1:T(8,128)} async-done(((f32[128,16,64]{0,2,1:T(8,128)}), f32[128,16,64]{0,2,1:T(8,128)}) %all-reduce.8.cloned.1.call-update) | async-done | bytes 524304 | tf_op jit(solution)/shard_map/psum | solution.py:154
  313.1 1.1 broadcast_divide_fusion
  314.4 0.8 copy.126
  315.3 4.5 gather_fusion.1
  319.8 7.6 %convolution_convert_fusion = bf16[1152,2048]{1,0:T(8,128)(2,1)S(1)} fusion(bf16[1152,1024]{1,0:T(8,128)(2,1)} %bitcast.106, bf16[1024,2048]{1,0:T(8,128)(2,1)} %param.13), kind=kOutput, calls=%fused_computation.10 | convolution fusion | flops 4834197504 | bytes 11272192 | tf_op jit(solution)/shard_map/dot_general | solution.py:108
  327.3 2.6 constant_dynamic-update-slice_fusion
  329.9 10.4 %fusion.61 = (bf16[6,512,1024]{2,1,0:T(8,128)(2,1)}, bf16[6,512,1024]{2,1,0:T(8,128)(2,1)}) fusion(bf16[6,512,2048]{2,1,0:T(8,128)(2,1)} %constant_dynamic-update-slice_fusion), kind=kLoop, calls=%fused_computation.103 | loop fusion | bytes 25165824 | tf_op jit(solution)/shard_map/slice | solution.py:131
  340.4 8.7 %copy.108 = bf16[6,512,1024]{1,2,0:T(8,128)(2,1)} copy(bf16[6,512,1024]{2,1,0:T(8,128)(2,1)} %get-tuple-element.46) | data formatting | bytes 12582912 | tf_op jit(solution)/shard_map/slice | solution.py:131
  349.0 8.8 %copy.107 = bf16[6,512,1024]{1,2,0:T(8,128)(2,1)} copy(bf16[6,512,1024]{2,1,0:T(8,128)(2,1)} %get-tuple-element.47) | data formatting | bytes 12582912 | tf_op jit(solution)/shard_map/slice | solution.py:132
  357.8 11.1 %fusion.67 = (f32[6,16,64]{2,1,0:T(8,128)S(1)}, f32[6,16,64,512]{3,2,1,0:T(8,128)}) fusion(pred[6,512]{1,0:T(8,128)(4,1)S(1)} %concatenate.31, bf16[6,512,16,64]{1,3,2,0:T(8,128)(2,1)} %bitcast.95, bf16[6,64,16,64]{3,2,1,0:T(8,128)(2,1)S(1)} %copy-done.7), kind=kOutput, calls=%fused_computation.109 | convolution fusion | flops 415236608 | bytes 19688448 | tf_op jit(solution)/shard_map/sub | solution.py:137
  368.9 8.3 %fusion.8 = bf16[6,16,64,64]{3,2,1,0:T(8,128)(2,1)S(1)} fusion(bf16[6,512,16,64]{1,3,2,0:T(8,128)(2,1)} %bitcast.96, f32[6,16,64,512]{3,2,1,0:T(8,128)} %get-tuple-element.67, f32[6,16,64]{2,1,0:T(8,128)S(1)} %get-tuple-element.66), kind=kOutput, calls=%fused_computation.16 | convolution fusion | flops 408944640 | bytes 19685376 | tf_op jit(solution)/shard_map/bhqk,bkhe->bqhe/dot_general | solution.py:139
  377.1 0.9 copy.125
  378.2 0.9 select_dynamic-update-slice_fusion
  379.2 4.3 convolution_convert_fusion.1
  383.6 0.4 copy.119
  384.0 0.5 copy-done.6
  384.5 3.7 bitcast_reduce_fusion.1
  388.2 59.0 %pmax.15 = f32[256,16]{0,1:T(8,128)S(1)} all-reduce(f32[256,16]{0,1:T(8,128)S(1)} %get-tuple-element.70), channel_id=1, replica_groups=mesh['groups'=2,'ctx'=16] {'ctx'}, use_global_device_ids=true, to_apply=%region_16.17 | all-reduce | flops 4096 | bytes 32768 | tf_op jit(solution)/shard_map/pmax | solution.py:170
  447.3 3.8 fusion.10
  451.1 0.4 copy.118
  451.5 7.1 %fusion.33 = f32[256,16,64]{0,2,1:T(8,128)} fusion(bf16[384,16,64]{0,2,1:T(8,128)(2,1)S(1)} %bitcast.104, f32[16,384,256]{2,1,0:T(8,128)} %get-tuple-element.71, f32[256,16]{0,1:T(8,128)S(1)} %get-tuple-element.70, f32[256,16]{0,1:T(8,128)S(1)} %get-tuple-element.41), kind=kOutput, calls=%fused_computation.42 | convolution fusion | flops 1211367424 | bytes 8159232 | tf_op jit(solution)/shard_map/qhk,khe->qhe/dot_general | solution.py:42
  458.7 57.9 %psum.71 = f32[256,16]{0,1:T(8,128)S(1)} all-reduce(f32[256,16]{0,1:T(8,128)S(1)} %get-tuple-element.40), channel_id=1, replica_groups=mesh['groups'=2,'ctx'=16] {'ctx'}, use_global_device_ids=true, to_apply=%region_19.20 | all-reduce | flops 4096 | bytes 32768 | tf_op jit(solution)/shard_map/psum | solution.py:173
  516.6 32.9 %all-reduce.10.cloned.1.call-done = f32[256,1024]{0,1:T(8,128)} async-done(((f32[256,1024]{0,1:T(8,128)}), f32[256,1024]{0,1:T(8,128)}) %all-reduce.10.cloned.1.call-update) | async-done | bytes 1048592 | tf_op jit(solution)/shard_map/psum | solution.py:173
  549.5 1.4 fusion.42
  550.9 0.7 copy.122
  (66 shorter events, 2.8 us)
Async XLA Ops:
  7.2 31.3 %copy-start = (bf16[384,1024]{1,0:T(8,128)(2,1)S(1)}, bf16[384,1024]{1,0:T(8,128)(2,1)}, u32[]{:S(2)}) copy-start(bf16[384,1024]{1,0:T(8,128)(2,1)} %param.16) | copy-start | bytes 2359300
  18.8 7.6 %copy-start.3 = (bf16[384,1024]{1,0:T(8,128)(2,1)S(1)}, bf16[384,1024]{1,0:T(8,128)(2,1)}, u32[]{:S(2)}) copy-start(bf16[384,1024]{1,0:T(8,128)(2,1)} %param.12) | copy-start | bytes 2359300
  18.8 296.5 %all-to-all-start = ((bf16[16,2,64,1024]{3,2,1,0:T(8,128)(2,1)}), bf16[16,2,64,1024]{3,2,1,0:T(8,128)(2,1)}, u32[]{:S(2)}, u32[]{:S(2)}) async-start(bf16[16,2,64,1024]{3,2,1,0:T(8,128)(2,1)} %broadcast_select_fusion), calls=%async_computation | async-start | bytes 8388608 | tf_op jit(solution)/shard_map/all_to_all | solution.py:102
  26.3 158.3 %all-reduce.12.cloned.1.call-start = ((), (), s32[]{:S(2)}) async-start(), calls=%async_computation.3 | async-start | bytes 1572864 | tf_op jit(solution)/shard_map/psum | solution.py:14
  27.0 25.6 %collective-permute-start = (bf16[64,1024]{1,0:T(8,128)(2,1)}, bf16[64,1024]{1,0:T(8,128)(2,1)S(1)}, u32[]{:S(2)}, u32[]{:S(2)}) collective-permute-start(bf16[64,1024]{1,0:T(8,128)(2,1)} %get-tuple-element.58), channel_id=1, source_target_pairs={{0,1},{1,2},{2,3},{3,4},{4,5},{5,6},{6,7},{7,8},{8,9},{9,10},{10,1... | collective-permute-start | bytes 393224 | tf_op jit(solution)/shard_map/ppermute | solution.py:24
  29.3 23.3 %collective-permute-start.1 = (bf16[64,1024]{1,0:T(8,128)(2,1)S(1)}, bf16[64,1024]{1,0:T(8,128)(2,1)S(1)}, u32[]{:S(2)}, u32[]{:S(2)}) collective-permute-start(bf16[64,1024]{1,0:T(8,128)(2,1)S(1)} %get-tuple-element.59), channel_id=1, source_target_pairs={{1,0},{2,1},{3,2},{4,3},{5,4},{6,5},{7,6},{8,7},{9,8},{10,9},{11,1... | collective-permute-start | bytes 393224 | tf_op jit(solution)/shard_map/ppermute | solution.py:25
  37.2 276.0 %all-reduce.8.cloned.1.call-start = ((), (), s32[]{:S(2)}) async-start(), calls=%async_computation.1 | async-start | bytes 1048576 | tf_op jit(solution)/shard_map/psum | solution.py:154
  40.6 5.5 copy-start.8
  46.0 6.5 %copy-start.11 = (s32[18]{0:T(128)S(1)}, s32[18]{0:T(128)}, u32[]{:S(2)}) copy-start(s32[18]{0:T(128)} %fusion.53) | copy-start | bytes 220
  184.7 37.1 %copy-start.5 = (bf16[384,1024]{0,1:T(8,128)(2,1)S(1)}, bf16[384,1024]{0,1:T(8,128)(2,1)}, u32[]{:S(2)}) copy-start(bf16[384,1024]{0,1:T(8,128)(2,1)} %copy.111) | copy-start | bytes 2359300
  219.1 2.8 copy-start.2
  219.1 5.4 copy-start.10
  222.0 5.7 %copy-start.4 = (f32[256,1024]{1,0:T(8,128)S(1)}, f32[256,1024]{1,0:T(8,128)}, u32[]{:S(2)}) copy-start(f32[256,1024]{1,0:T(8,128)} %convert_select_fusion) | copy-start | bytes 3145732
  224.5 324.9 %all-reduce.10.cloned.1.call-start = ((), (), s32[]{:S(2)}) async-start(), calls=%async_computation.2 | async-start | bytes 2097152 | tf_op jit(solution)/shard_map/psum | solution.py:173
  349.0 8.8 %copy-start.7 = (bf16[6,64,16,64]{3,2,1,0:T(8,128)(2,1)S(1)}, bf16[6,64,16,64]{3,2,1,0:T(8,128)(2,1)}, u32[]{:S(2)}) copy-start(bf16[6,64,16,64]{3,2,1,0:T(8,128)(2,1)} %reshape.293) | copy-start | bytes 2359300
  379.2 4.3 copy-start.9
  383.5 1.0 copy-start.6
  451.5 100.1 %copy-start.1 = (bf16[384,1024]{1,0:T(8,128)(2,1)S(1)}, bf16[384,1024]{1,0:T(8,128)(2,1)}, u32[]{:S(2)}) copy-start(bf16[384,1024]{1,0:T(8,128)(2,1)} %param.16) | copy-start | bytes 2359300
Sparse Core Ops, SparseCore 0:
  37.3 147.3 all-reduce.11
  224.6 88.4 all-reduce.7
  458.8 90.5 all-reduce.9
where the time goes:
time: 560 us; the launch traced here: 558 us
  blocking collectives  219 us (39%)
  waiting for transfers between devices  171 us (31%)
  local copies, waits for them, and re-layouts  62.3 us (11%)
  matrix products  53.8 us (10%)
  other arithmetic  26.9 us (5%)
  between operations  14.2 us (3%)
  starting transfers between devices  11.2 us (2%)
    psum x1, waiting for transfers between devices, from_root(): return lax.psum(block, axis)  125 us
    psum x1, blocking collectives, local(): lax.psum((rescale(end_sums, end_scale), end_totals * end_scale, looked),...  70.7 us
    pmax x1, blocking collectives, local(): top_scores = lax.pmax(cross_peak, 'ctx')  59 us
    psum x1, blocking collectives, local(): lax.psum((scaled_sums, cross_totals * scaling), 'ctx')  57.9 us
    psum x1, waiting for transfers between devices, local(): lax.psum((scaled_sums, cross_totals * scaling), 'ctx')  32.9 us
    pmax x1, blocking collectives, local(): end_top = lax.pmax(end_peak, 'ctx')  30.9 us
    slice x2, local copies, waits for them, and re-layouts, local(): key_sets[:, :, :feature_count].reshape(block_count, span, HEADS, HEAD)  19.1 us
    psum x1, waiting for transfers between devices, local(): lax.psum((rescale(end_sums, end_scale), end_totals * end_scale, looked),...  13.7 us
  transfers between devices with their start and end apart: 6, of which 3 were waited for; matrix products, arithmetic and copies ran while one was open for 8% of the time, Pallas kernels for 0%

commit v1 on v0

--- a/solution.py
+++ b/solution.py
@@ -11,7 +11,7 @@
 
 def from_root(block, axis, holder):
     block = jnp.where(lax.axis_index(axis) == holder, block, jnp.zeros_like(block))
-    return lax.psum(block, axis)
+    return jnp.sum(lax.all_gather(block, axis), axis=0)
 
 
 def padded_2(x, sides, width):

time: 560 us -> 640 us (1.14)
  blocking collectives: 219 us -> 292 us
  other arithmetic: 26.9 us -> 34.4 us
    all_gather x0 -> x4, waiting for transfers between devices: none -> 138 us  [from_root(): return jnp.sum(lax.all_gather(block, axis), axis=0)]
    psum x1 -> x0, waiting for transfers between devices: 125 us -> none  [from_root(): return lax.psum(block, axis)]
    psum x1, blocking collectives: 70.7 us -> 143 us  [local(): lax.psum((rescale(end_sums, end_scale), end_totals * end_scale, looked),...]
    psum x1, waiting for transfers between devices: 13.7 us -> 0.01 us  [local(): lax.psum((rescale(end_sums, end_scale), end_totals * end_scale, looked),...]
    reduce_sum x0 -> x4, other arithmetic: none -> 9.93 us  [from_root(): return jnp.sum(lax.all_gather(block, axis), axis=0)]
  transfers between devices with their start and end apart: 6 -> 9, of which waited for: 3 -> 5; matrix products, arithmetic and copies ran while one was open for 8% -> 8% of each run, Pallas kernels for 0% -> 0%
where the time goes in v1:
time: 640 us; the launch traced here: 638 us
  blocking collectives  292 us (46%)
  waiting for transfers between devices  172 us (27%)
  local copies, waits for them, and re-layouts  61.6 us (10%)
  matrix products  55.2 us (9%)
  other arithmetic  34.4 us (5%)
  between operations  14.5 us (2%)
  starting transfers between devices  9.1 us (1%)
    psum x1, blocking collectives, local(): lax.psum((rescale(end_sums, end_scale), end_totals * end_scale, looked),...  143 us
    all_gather x4, waiting for transfers between devices, from_root(): return jnp.sum(lax.all_gather(block, axis), axis=0)  138 us
    pmax x1, blocking collectives, local(): top_scores = lax.pmax(cross_peak, 'ctx')  58.3 us
    psum x1, blocking collectives, local(): lax.psum((scaled_sums, cross_totals * scaling), 'ctx')  58.2 us
    psum x1, waiting for transfers between devices, local(): lax.psum((scaled_sums, cross_totals * scaling), 'ctx')  32.7 us
    pmax x1, blocking collectives, local(): end_top = lax.pmax(end_peak, 'ctx')  31.9 us
    slice x2, local copies, waits for them, and re-layouts, local(): key_sets[:, :, :feature_count].reshape(block_count, span, HEADS, HEAD)  19.3 us
  transfers between devices with their start and end apart: 9, of which 5 were waited for; matrix products, arithmetic and copies ran while one was open for 8% of the time, Pallas kernels for 0%

profile of v1, /device:TPU:0, one launch (start us, length us, event | category | flops | bytes accessed | tf_op | source)
XLA Modules:
  0.0 638.3 jit_solution(1760254359267304034)
XLA Ops:
  7.2 1.8 slice_select_fusion.4
  9.1 0.7 all-gather.13.cloned.1.call-update
  9.8 4.2 convolution_convert_fusion.2
  14.1 1.0 fusion.63
  15.1 1.2 copy.126
  16.2 1.5 copy.127
  17.7 36.6 %all-gather.15.cloned.1.call-done = bf16[1024,1024]{1,0:T(8,128)(2,1)} async-done(((bf16[64,1024]{1,0:T(8,128)(2,1)}), bf16[1024,1024]{1,0:T(8,128)(2,1)}) %all-gather.15.cloned.1.call-update) | async-done | bytes 2097168 | tf_op jit(solution)/shard_map/all_gather | solution.py:14
  54.3 2.0 reduce_sum.102
  56.3 40.4 %all-gather.13.cloned.1.call-done = bf16[1024,1024]{1,0:T(8,128)(2,1)} async-done(((bf16[64,1024]{1,0:T(8,128)(2,1)}), bf16[1024,1024]{1,0:T(8,128)(2,1)}) %all-gather.13.cloned.1.call-update) | async-done | bytes 2097168 | tf_op jit(solution)/shard_map/all_gather | solution.py:14
  96.7 2.0 reduce_sum.101
  98.7 0.7 pad_maximum_fusion.3
  99.4 1.1 copy.128
  100.5 2.3 bitcast_reduce_fusion.2
  102.8 31.9 %pmax.14 = f32[128,16]{0,1:T(8,128)S(1)} all-reduce(f32[128,16]{0,1:T(8,128)S(1)} %get-tuple-element.66), channel_id=1, replica_groups=mesh['groups'=2,'ctx'=16] {'ctx'}, use_global_device_ids=true, to_apply=%region_10.11 | all-reduce | flops 2048 | bytes 16384 | tf_op jit(solution)/shard_map/pmax | solution.py:152
  134.8 2.6 fusion.18
  137.4 0.6 fusion.60
  138.0 3.7 fusion.39
  141.7 0.8 slice_select_fusion.2
  145.1 2.7 gather_fusion
  147.8 4.5 broadcast_select_fusion
  152.3 4.5 all-to-all-start
  156.9 0.7 fusion.64
  157.6 1.3 collective-permute-start.1
  158.9 3.0 collective-permute-start
  161.9 0.6 pad.8.clone
  162.5 0.7 compare_select_fusion
  163.2 0.6 pad_clamp_fusion
  163.8 2.1 gather_fusion.2
  165.9 0.7 compare_and_fusion
  166.6 0.7 pad_add_fusion
  167.3 2.2 convert_select_fusion
  169.6 3.2 reshape.293
  173.0 2.9 convolution_convert_fusion.3
  176.4 1.3 constant_dynamic-update-slice_fusion.3
  177.7 1.3 constant_dynamic-update-slice_fusion.2
  179.0 1.4 constant_dynamic-update-slice_fusion.1
  180.4 143.5 %all-reduce.9 = (f32[128,16]{0,1:T(8,128)S(1)}, bf16[256,1024]{1,0:T(8,128)(2,1)S(1)}) all-reduce(f32[128,16]{0,1:T(8,128)S(1)} %copy-done.7, f32[256,1024]{1,0:T(8,128)} %convert_select_fusion), channel_id=1, replica_groups=mesh['groups'=2,'ctx'=16] {'ctx'}, use_global_device_ids=true, to_apply=%region_13.14 | all-reduce | flops 264192 | bytes 1589248 | tf_op jit(solution)/shard_map/psum | solution.py:154
  323.9 1.0 copy.135
  324.9 1.1 broadcast_divide_fusion
  326.2 0.8 copy.141
  327.1 12.2 %all-gather.11.cloned.1.call-done = bf16[1024,2048]{1,0:T(8,128)(2,1)} async-done(((bf16[64,2048]{1,0:T(8,128)(2,1)}), bf16[1024,2048]{1,0:T(8,128)(2,1)}) %all-gather.11.cloned.1.call-update) | async-done | bytes 4194320 | tf_op jit(solution)/shard_map/all_gather | solution.py:14
  339.3 3.0 reduce_sum.96
  342.3 48.4 %all-gather.9.cloned.1.call-done = bf16[1024,2048]{1,0:T(8,128)(2,1)} async-done(((bf16[64,2048]{1,0:T(8,128)(2,1)}), bf16[1024,2048]{1,0:T(8,128)(2,1)}) %all-gather.9.cloned.1.call-update) | async-done | bytes 4194320 | tf_op jit(solution)/shard_map/all_gather | solution.py:14
  390.7 3.0 reduce_sum.95
  393.7 4.5 gather_fusion.1
  398.2 7.6 %convolution_convert_fusion = bf16[1152,2048]{1,0:T(8,128)(2,1)S(1)} fusion(bf16[1152,1024]{1,0:T(8,128)(2,1)} %bitcast.112, bf16[1024,2048]{1,0:T(8,128)(2,1)} %param.13), kind=kOutput, calls=%fused_computation.10 | convolution fusion | flops 4834197504 | bytes 11272192 | tf_op jit(solution)/shard_map/dot_general | solution.py:108
  405.9 2.1 broadcast_dynamic-update-slice_fusion
  408.0 2.6 constant_dynamic-update-slice_fusion
  410.5 10.5 %fusion.61 = (bf16[6,512,1024]{2,1,0:T(8,128)(2,1)}, bf16[6,512,1024]{2,1,0:T(8,128)(2,1)}) fusion(bf16[6,512,2048]{2,1,0:T(8,128)(2,1)} %constant_dynamic-update-slice_fusion), kind=kLoop, calls=%fused_computation.103 | loop fusion | bytes 25165824 | tf_op jit(solution)/shard_map/slice | solution.py:131
  421.0 8.7 %copy.122 = bf16[6,512,1024]{1,2,0:T(8,128)(2,1)} copy(bf16[6,512,1024]{2,1,0:T(8,128)(2,1)} %get-tuple-element.45) | data formatting | bytes 12582912 | tf_op jit(solution)/shard_map/slice | solution.py:132
  429.7 8.8 %copy.123 = bf16[6,512,1024]{1,2,0:T(8,128)(2,1)} copy(bf16[6,512,1024]{2,1,0:T(8,128)(2,1)} %get-tuple-element.44) | data formatting | bytes 12582912 | tf_op jit(solution)/shard_map/slice | solution.py:131
  438.4 11.1 %fusion.67 = (f32[6,16,64]{2,1,0:T(8,128)S(1)}, f32[6,16,64,512]{3,2,1,0:T(8,128)}) fusion(pred[6,512]{1,0:T(8,128)(4,1)S(1)} %concatenate.31, bf16[6,512,16,64]{1,3,2,0:T(8,128)(2,1)} %bitcast.100, bf16[6,64,16,64]{3,2,1,0:T(8,128)(2,1)S(1)} %copy-done.5), kind=kOutput, calls=%fused_computation.109 | convolution fusion | flops 415236608 | bytes 19688448 | tf_op jit(solution)/shard_map/sub | solution.py:137
  449.5 8.3 %fusion.8 = bf16[6,16,64,64]{3,2,1,0:T(8,128)(2,1)S(1)} fusion(bf16[6,512,16,64]{1,3,2,0:T(8,128)(2,1)} %bitcast.99, f32[6,16,64,512]{3,2,1,0:T(8,128)} %get-tuple-element.65, f32[6,16,64]{2,1,0:T(8,128)S(1)} %get-tuple-element.64), kind=kOutput, calls=%fused_computation.16 | convolution fusion | flops 408944640 | bytes 19685376 | tf_op jit(solution)/shard_map/bhqk,bkhe->bqhe/dot_general | solution.py:139
  457.8 0.7 copy.140
  458.6 0.9 select_dynamic-update-slice_fusion
  459.7 4.3 convolution_convert_fusion.1
  465.0 3.7 bitcast_reduce_fusion.1
  468.7 58.3 %pmax.15 = f32[256,16]{0,1:T(8,128)S(1)} all-reduce(f32[256,16]{0,1:T(8,128)S(1)} %get-tuple-element.68), channel_id=1, replica_groups=mesh['groups'=2,'ctx'=16] {'ctx'}, use_global_device_ids=true, to_apply=%region_16.17 | all-reduce | flops 4096 | bytes 32768 | tf_op jit(solution)/shard_map/pmax | solution.py:170
  526.9 3.8 fusion.10
  531.2 7.2 %fusion.33 = f32[256,16,64]{0,2,1:T(8,128)} fusion(bf16[384,16,64]{0,2,1:T(8,128)(2,1)S(1)} %bitcast.110, f32[16,384,256]{2,1,0:T(8,128)} %get-tuple-element.69, f32[256,16]{0,1:T(8,128)S(1)} %get-tuple-element.68, f32[256,16]{0,1:T(8,128)S(1)} %get-tuple-element.39), kind=kOutput, calls=%fused_computation.42 | convolution fusion | flops 1211367424 | bytes 8159232 | tf_op jit(solution)/shard_map/qhk,khe->qhe/dot_general | solution.py:42
  538.4 58.2 %psum.39 = f32[256,16]{0,1:T(8,128)S(1)} all-reduce(f32[256,16]{0,1:T(8,128)S(1)} %get-tuple-element.38), channel_id=1, replica_groups=mesh['groups'=2,'ctx'=16] {'ctx'}, use_global_device_ids=true, to_apply=%region_19.20 | all-reduce | flops 4096 | bytes 32768 | tf_op jit(solution)/shard_map/psum | solution.py:173
  596.5 32.7 %all-reduce.8.cloned.1.call-done = f32[256,1024]{0,1:T(8,128)} async-done(((f32[256,1024]{0,1:T(8,128)}), f32[256,1024]{0,1:T(8,128)}) %all-reduce.8.cloned.1.call-update) | async-done | bytes 1048592 | tf_op jit(solution)/shard_map/psum | solution.py:173
  629.3 1.4 fusion.42
  630.7 0.7 copy.137
  (73 shorter events, 5.3 us)
Async XLA Ops:
  7.2 156.7 %copy-start = (bf16[384,1024]{1,0:T(8,128)(2,1)S(1)}, bf16[384,1024]{1,0:T(8,128)(2,1)}, u32[]{:S(2)}) copy-start(bf16[384,1024]{1,0:T(8,128)(2,1)} %param.16) | copy-start | bytes 2359300
  7.2 47.1 %all-gather.15.cloned.1.call-start = ((), (), s32[]{:S(2)}) async-start(), calls=%async_computation.6 | async-start | bytes 2228224 | tf_op jit(solution)/shard_map/all_gather | solution.py:14
  9.0 87.6 %all-gather.13.cloned.1.call-start = ((), (), s32[]{:S(2)}) async-start(), calls=%async_computation.5 | async-start | bytes 2228224 | tf_op jit(solution)/shard_map/all_gather | solution.py:14
  9.8 315.2 %all-reduce.6.cloned.1.call-start = ((), (), s32[]{:S(2)}) async-start(), calls=%async_computation.1 | async-start | bytes 1048576 | tf_op jit(solution)/shard_map/psum | solution.py:154
  134.8 3.2 copy-start.2
  134.8 8.4 %copy-start.8 = (s32[96,3]{0,1:T(4,128)S(1)}, s32[96,3]{0,1:T(4,128)}, u32[]{:S(2)}) copy-start(s32[96,3]{0,1:T(4,128)} %param.14) | copy-start | bytes 3460
  137.4 7.7 %copy-start.3 = (bf16[384,1024]{1,0:T(8,128)(2,1)S(1)}, bf16[384,1024]{1,0:T(8,128)(2,1)}, u32[]{:S(2)}) copy-start(bf16[384,1024]{1,0:T(8,128)(2,1)} %param.12) | copy-start | bytes 2359300
  141.7 197.6 %all-gather.11.cloned.1.call-start = ((), (), s32[]{:S(2)}) async-start(), calls=%async_computation.4 | async-start | bytes 4456448 | tf_op jit(solution)/shard_map/all_gather | solution.py:14
  142.6 248.1 %all-gather.9.cloned.1.call-start = ((), (), s32[]{:S(2)}) async-start(), calls=%async_computation.3 | async-start | bytes 4456448 | tf_op jit(solution)/shard_map/all_gather | solution.py:14
  152.3 241.4 %all-to-all-start = ((bf16[16,2,64,1024]{3,2,1,0:T(8,128)(2,1)}), bf16[16,2,64,1024]{3,2,1,0:T(8,128)(2,1)}, u32[]{:S(2)}, u32[]{:S(2)}) async-start(bf16[16,2,64,1024]{3,2,1,0:T(8,128)(2,1)} %broadcast_select_fusion), calls=%async_computation | async-start | bytes 8388608 | tf_op jit(solution)/shard_map/all_to_all | solution.py:102
  156.9 472.4 %all-reduce.8.cloned.1.call-start = ((), (), s32[]{:S(2)}) async-start(), calls=%async_computation.2 | async-start | bytes 2097152 | tf_op jit(solution)/shard_map/psum | solution.py:173
  157.6 15.4 %collective-permute-start.1 = (bf16[64,1024]{1,0:T(8,128)(2,1)}, bf16[64,1024]{1,0:T(8,128)(2,1)S(1)}, u32[]{:S(2)}, u32[]{:S(2)}) collective-permute-start(bf16[64,1024]{1,0:T(8,128)(2,1)} %get-tuple-element.57), channel_id=1, source_target_pairs={{1,0},{2,1},{3,2},{4,3},{5,4},{6,5},{7,6},{8,7},{9,8},{10,9},{11,1... | collective-permute-start | bytes 393224 | tf_op jit(solution)/shard_map/ppermute | solution.py:25
  158.9 14.1 %collective-permute-start = (bf16[64,1024]{1,0:T(8,128)(2,1)S(1)}, bf16[64,1024]{1,0:T(8,128)(2,1)S(1)}, u32[]{:S(2)}, u32[]{:S(2)}) collective-permute-start(bf16[64,1024]{1,0:T(8,128)(2,1)S(1)} %get-tuple-element.56), channel_id=1, source_target_pairs={{0,1},{1,2},{2,3},{3,4},{4,5},{5,6},{6,7},{7,8},{8,9},{9,10},{10,1... | collective-permute-start | bytes 393224 | tf_op jit(solution)/shard_map/ppermute | solution.py:24
  176.4 4.1 copy-start.7
  429.7 8.8 %copy-start.5 = (bf16[6,64,16,64]{3,2,1,0:T(8,128)(2,1)S(1)}, bf16[6,64,16,64]{3,2,1,0:T(8,128)(2,1)}, u32[]{:S(2)}) copy-start(bf16[6,64,16,64]{3,2,1,0:T(8,128)(2,1)} %reshape.293) | copy-start | bytes 2359300
  459.7 4.3 copy-start.6
  464.0 1.0 copy-start.4
  531.2 100.3 %copy-start.1 = (bf16[384,1024]{1,0:T(8,128)(2,1)S(1)}, bf16[384,1024]{1,0:T(8,128)(2,1)}, u32[]{:S(2)}) copy-start(bf16[384,1024]{1,0:T(8,128)(2,1)} %param.16) | copy-start | bytes 2359300
Sparse Core Ops, SparseCore 0:
  10.2 44.0 all-gather.14
  56.5 40.1 all-gather.12
  141.8 139.9 all-reduce.5
  283.8 55.4 all-gather.10
  341.3 49.3 all-gather.8
  538.5 90.7 all-reduce.7
